TPU v7x, 32 devices: a whole 2x2x4 slice. The times are simulated.
32 devices in a mesh: groups: 2 (over y), seq: 4 (over z), head: 2 (over x), sub: 2 (over core).
Axes of the slice: x: 2, y: 2, z: 4, core: 2. Of those that a mesh axis runs over, the one named last changes fastest.
Arguments:
- tokens: int32 [3, 4096], P(None, ('groups', 'seq')), parts along dimension 1, may hold values from 0 to 1023
- masked: int32 [4096], P(('groups', 'seq')), parts along dimension 0, may hold values 0 or 1
- used_frames: int32 [2], P('groups'), parts along dimension 0, may hold values from 1024 to 2048
- tables: bfloat16 [3, 1024, 1024], P(None, None, ('head', 'sub')), may hold values from -6 to 6
- mask_vec: bfloat16 [1024], P(('head', 'sub')), may hold values from -6 to 6
- attn_in: bfloat16 [3, 1024, 512], P(None, None, ('head', 'sub')), may hold values from -0.1875 to 0.1875
- head_temp: float32 [8], P(('head', 'sub')), may hold values from 12 to 28
- attn_out: bfloat16 [512, 1024], P(('head', 'sub')), may hold values from -0.25 to 0.25
- conv_in: bfloat16 [2, 1024, 1024], P(None, None, ('head', 'sub')), may hold values from -0.1875 to 0.1875
- conv_kernel: float32 [31, 1024], P(None, ('head', 'sub')), may hold values from -1 to 1
- conv_out: bfloat16 [1024, 1024], P(('head', 'sub')), may hold values from -0.1875 to 0.1875
- voc_in: bfloat16 [1024, 512], P(('head', 'sub')), may hold values from -0.1875 to 0.1875
- voc_kernel: float32 [7, 512], replicated, may hold values from -2 to 2
- voc_up: bfloat16 [512, 1536], P(('head', 'sub')), may hold values from -0.25 to 0.25
- voc_down: bfloat16 [1536, 512], P(('head', 'sub')), may hold values from -0.15625 to 0.15625
- voc_head: bfloat16 [512, 1282], P(('head', 'sub')), may hold values from -0.25 to 0.25
- head_bias: float32 [1282], replicated, may hold values from 0.5 to 2.5
Outputs:
- features: bfloat16 [4096, 1024], P(('groups', 'seq', 'head', 'sub')), parts along dimension 0
- waveform: float32 [1310720], P(('groups', 'seq', 'head', 'sub')), parts along dimension 0
There are 2 independent parts, one for each index of `groups`. A program takes and returns all parts, laid end to end along the dimension named above; an argument that names none is the same for every part. Nothing has to cross between parts.
All inputs are finite; a program needn't handle non-finite values. No bound on the sum of `masked` on one device may be relied on, other than what follows from the above.
Results may differ from a plain program's by a relative error of at most 0.02.
Values may be sent and summed in bfloat16 or wider, within the bound.
A program may use at most 64 MiB of HBM per device.

v0:
```python
import math
import jax
import jax.numpy as jnp
from jax import lax
from jax.sharding import PartitionSpec as P

HOP = 320


def with_halo(x, sides, width):
    for axis, dim in sides:
        size, length = (lax.axis_size(axis), x.shape[dim])
        up = [(i, (i + 1) % size) for i in range(size - 1)]
        down = [(j, i) for i, j in up]
        last = lax.slice_in_dim(x, length - width, length, axis=dim)
        initial = lax.slice_in_dim(x, 0, width, axis=dim)
        before = lax.ppermute(last, axis, up)
        after = lax.ppermute(initial, axis, down)
        x = jnp.concatenate([before, x, after], axis=dim)
    return x


def layer_norm(values):
    average = jnp.mean(values, axis=-1, keepdims=True)
    centered = values - average
    return centered * lax.rsqrt(jnp.mean(centered * centered, axis=-1, keepdims=True) + 1e-05)


def unit_heads(projected, head_count):
    row_count = projected.shape[0]
    split_heads = projected.reshape(row_count, head_count, projected.shape[1] // head_count)
    scaled = split_heads * lax.rsqrt(
        jnp.sum(split_heads * split_heads, axis=-1, keepdims=True) + 1e-06
    )
    return scaled.astype(jnp.bfloat16)


def depthwise(kernel, padded_rows):
    tap_count = kernel.shape[0]
    out_rows = padded_rows.shape[0] - tap_count + 1
    result = jnp.zeros((out_rows, padded_rows.shape[1]), jnp.float32)
    for offset in range(tap_count):
        result = result + kernel[offset] * padded_rows[offset : offset + out_rows].astype(
            jnp.float32
        )
    return result


def attend_block(
    paired_sums,
    key_tile_rows,
    value_tile_rows,
    leading_row,
    query_normalized,
    similarity_sharpness,
    frame_ceiling,
):
    weighted, normalizer = paired_sums
    row_count = key_tile_rows.shape[0]
    angular_similarity = jnp.einsum(
        "qhd,khd->hqk", query_normalized, key_tile_rows, preferred_element_type=jnp.float32
    )
    token_position = leading_row + lax.broadcasted_iota(jnp.int32, (1, 1, row_count), 2)
    attention_probabilities = jnp.where(
        token_position < frame_ceiling,
        jnp.exp(similarity_sharpness[:, None, None] * (angular_similarity - 1.0)),
        0.0,
    )
    normalizer = normalizer + jnp.sum(attention_probabilities, axis=2).T
    weighted = weighted + jnp.einsum(
        "hqk,khd->qhd",
        attention_probabilities.astype(jnp.bfloat16),
        value_tile_rows,
        preferred_element_type=jnp.float32,
    )
    return (weighted, normalizer)


def synthesis_tables(bin_count, fft_size):
    bin_ids = lax.broadcasted_iota(jnp.int32, (bin_count, fft_size), 0)
    sample_ids = lax.broadcasted_iota(jnp.int32, (bin_count, fft_size), 1)
    phase_angle = 2.0 * math.pi / fft_size * (bin_ids * sample_ids % fft_size).astype(jnp.float32)
    edge_bin = (bin_ids == 0) | (bin_ids == bin_count - 1)
    factor = jnp.where(edge_bin, 1.0, 2.0) / fft_size
    cos_table = factor * jnp.cos(phase_angle)
    sin_table = jnp.where(edge_bin, 0.0, -factor * jnp.sin(phase_angle))
    return jnp.concatenate([cos_table, sin_table], axis=0)


def local(
    tokens,
    masked,
    used_frames,
    tables,
    mask_vec,
    attn_in,
    head_temp,
    attn_out,
    conv_in,
    conv_kernel,
    conv_out,
    voc_in,
    voc_kernel,
    voc_up,
    voc_down,
    voc_head,
    head_bias,
):
    frame_count = tokens.shape[1]
    group_count = lax.axis_size(("head", "sub"))
    group_index = lax.axis_index(("head", "sub"))
    seq_index = lax.axis_index("seq")
    slab_rows = frame_count // group_count
    frame_ceiling = used_frames[0]
    total_frames = frame_count * lax.axis_size("seq")
    code_ids = lax.broadcasted_iota(jnp.int32, (frame_count, tables.shape[1]), 1)
    masked_rows = masked == 1
    embedded = masked_rows.astype(jnp.float32)[:, None] * mask_vec.astype(jnp.float32)[None, :]
    for rvq_level in range(3):
        matches = tokens[rvq_level][:, None] == code_ids
        if rvq_level == 2:
            matches = matches & jnp.logical_not(masked_rows)[:, None]
        embedded = embedded + jnp.dot(
            matches.astype(jnp.bfloat16), tables[rvq_level], preferred_element_type=jnp.float32
        )
    embedded = embedded.astype(jnp.bfloat16)
    inputs, voc_in_full, voc_up_full, voc_down_full, voc_head_full = (
        lax.all_gather(embedded, ("head", "sub"), axis=1, tiled=True),
        lax.all_gather(voc_in, ("head", "sub"), axis=0, tiled=True),
        lax.all_gather(voc_up, ("head", "sub"), axis=0, tiled=True),
        lax.all_gather(voc_down, ("head", "sub"), axis=0, tiled=True),
        lax.all_gather(voc_head, ("head", "sub"), axis=0, tiled=True),
    )
    normed = layer_norm(inputs.astype(jnp.float32)).astype(jnp.bfloat16)
    local_heads = head_temp.shape[0]
    query_normalized = unit_heads(
        jnp.dot(normed, attn_in[0], preferred_element_type=jnp.float32), local_heads
    )
    key_unit = unit_heads(
        jnp.dot(normed, attn_in[1], preferred_element_type=jnp.float32), local_heads
    ).reshape(frame_count, -1)
    value_rows = jnp.dot(normed, attn_in[2], preferred_element_type=jnp.float32).astype(
        jnp.bfloat16
    )
    head_size = value_rows.shape[1] // local_heads
    start_pair = (
        jnp.zeros((frame_count, local_heads, head_size), jnp.float32),
        jnp.zeros((frame_count, local_heads), jnp.float32),
    )
    paired_sums = start_pair
    key_piece = lax.all_gather(key_unit, "seq", axis=0, tiled=True)
    value_piece = lax.all_gather(value_rows, "seq", axis=0, tiled=True)
    row_count = key_piece.shape[0]
    key_heads = key_piece.reshape(row_count, local_heads, head_size)
    value_heads = value_piece.reshape(row_count, local_heads, head_size)
    block_count = row_count // 512

    def scan_step(inner_pair, block_item):
        key_tile_rows, value_tile_rows, block_index = block_item
        return (
            attend_block(
                inner_pair,
                key_tile_rows,
                value_tile_rows,
                block_index * 512,
                query_normalized,
                head_temp,
                frame_ceiling,
            ),
            None,
        )

    block_items = (
        key_heads.reshape(block_count, 512, local_heads, head_size),
        value_heads.reshape(block_count, 512, local_heads, head_size),
        jnp.arange(block_count, dtype=jnp.int32),
    )
    paired_sums, _unused = lax.scan(scan_step, paired_sums, block_items)
    weighted, normalizer = paired_sums
    attended = (weighted / normalizer[:, :, None]).reshape(frame_count, -1).astype(jnp.bfloat16)
    head_part = jnp.dot(attended, attn_out, preferred_element_type=jnp.float32)
    fft_size = 2 * (head_bias.shape[0] // 2 - 1)
    intersection = fft_size // HOP
    half_voc = voc_kernel.shape[0] // 2
    vocoder_rim = half_voc + intersection // 2
    conv_reach = conv_kernel.shape[0] // 2 + vocoder_rim
    window_rows = slab_rows + 2 * vocoder_rim
    stream = inputs.astype(jnp.float32) + lax.psum(
        head_part.astype(jnp.bfloat16), ("head", "sub")
    ).astype(jnp.float32)
    stream_rims = with_halo(stream.astype(jnp.bfloat16), (("seq", 0),), conv_reach).astype(
        stream.dtype
    )
    conv_normed = layer_norm(stream_rims).astype(jnp.bfloat16)
    residual_window = lax.dynamic_slice_in_dim(
        stream_rims, group_index * slab_rows + conv_reach - vocoder_rim, window_rows, 0
    )
    gate_value = jnp.dot(conv_normed, conv_in[0], preferred_element_type=jnp.float32)
    gate_signal = jnp.dot(conv_normed, conv_in[1], preferred_element_type=jnp.float32)
    gated_rows = (gate_value * jax.nn.sigmoid(gate_signal)).astype(jnp.bfloat16)
    depth_rows = depthwise(conv_kernel, gated_rows)
    activated = (depth_rows * jax.nn.sigmoid(depth_rows)).astype(jnp.bfloat16)
    windows = jnp.stack(
        [
            activated[member * slab_rows : member * slab_rows + window_rows]
            for member in range(group_count)
        ]
    )
    partial_out = jnp.einsum("gsc,cd->gsd", windows, conv_out, preferred_element_type=jnp.float32)
    conv_sum = lax.psum_scatter(
        partial_out.astype(jnp.bfloat16), ("head", "sub"), scatter_dimension=0, tiled=True
    ).astype(jnp.float32)[0]
    block_norm = layer_norm(residual_window + conv_sum).astype(jnp.bfloat16)
    feature_out = block_norm[vocoder_rim : vocoder_rim + slab_rows]
    first_frame = seq_index * frame_count + group_index * slab_rows - vocoder_rim
    frame_ids = first_frame + lax.broadcasted_iota(jnp.int32, (window_rows, 1), 0)
    live_rows = (frame_ids >= 0) & (frame_ids < frame_ceiling)
    base_rows = layer_norm(
        jnp.where(
            live_rows, jnp.dot(block_norm, voc_in_full, preferred_element_type=jnp.float32), 0.0
        )
    )
    vdepth = depthwise(voc_kernel, base_rows)
    voc_rows = vdepth.shape[0]
    inner_rows = layer_norm(vdepth).astype(jnp.bfloat16)
    hidden = jax.nn.gelu(
        jnp.dot(inner_rows, voc_up_full, preferred_element_type=jnp.float32), approximate=False
    ).astype(jnp.bfloat16)
    refined = base_rows[half_voc : half_voc + voc_rows] + jnp.dot(
        hidden, voc_down_full, preferred_element_type=jnp.float32
    )
    head_input = layer_norm(refined).astype(jnp.bfloat16)
    spectrum = jnp.dot(head_input, voc_head_full, preferred_element_type=jnp.float32) + head_bias
    bin_count = spectrum.shape[1] // 2
    magnitude = jnp.minimum(jnp.exp(spectrum[:, :bin_count]), 100.0)
    phase_rows = spectrum[:, bin_count:]
    coefficients = jnp.concatenate(
        [magnitude * jnp.cos(phase_rows), magnitude * jnp.sin(phase_rows)], axis=1
    )
    wave_rows = jnp.dot(
        coefficients, synthesis_tables(bin_count, fft_size), precision=lax.Precision.HIGHEST
    )
    sample_ids = lax.broadcasted_iota(jnp.int32, (fft_size,), 0).astype(jnp.float32)
    hann_window = 0.5 - 0.5 * jnp.cos(2.0 * math.pi / fft_size * sample_ids)
    wave_ids = first_frame + half_voc + lax.broadcasted_iota(jnp.int32, (voc_rows, 1), 0)
    exists = ((wave_ids >= 0) & (wave_ids < total_frames)).astype(jnp.float32)
    framed = (wave_rows * hann_window[None, :] * exists).reshape(voc_rows, intersection, HOP)
    env_rows = (exists * (hann_window * hann_window)[None, :]).reshape(voc_rows, intersection, HOP)
    audio_sum = jnp.zeros((slab_rows, HOP), jnp.float32)
    energy = jnp.zeros((slab_rows, HOP), jnp.float32)
    for quarter in range(intersection):
        begin = intersection - quarter
        audio_sum = audio_sum + framed[begin : begin + slab_rows, quarter]
        energy = energy + env_rows[begin : begin + slab_rows, quarter]
    waveform = (audio_sum / energy).reshape(slab_rows * HOP)
    return (feature_out, waveform)


def solution(mesh):
    in_specs = (
        P(None, ("groups", "seq")),
        P(("groups", "seq")),
        P("groups"),
        P(None, None, ("head", "sub")),
        P(("head", "sub")),
        P(None, None, ("head", "sub")),
        P(("head", "sub")),
        P(("head", "sub"), None),
        P(None, None, ("head", "sub")),
        P(None, ("head", "sub")),
        P(("head", "sub"), None),
        P(("head", "sub"), None),
        P(),
        P(("head", "sub"), None),
        P(("head", "sub"), None),
        P(("head", "sub"), None),
        P(),
    )
    out_specs = (P(("groups", "seq", "head", "sub"), None), P(("groups", "seq", "head", "sub")))
    return jax.shard_map(local, mesh=mesh, in_specs=in_specs, out_specs=out_specs, check_vma=False)
```

profile of v0, /device:TPU:0, one launch (start us, length us, event | category | flops | bytes accessed | tf_op | source)
XLA Modules:
  0.0 276.2 jit_solution(7080855097597714248)
XLA Ops:
  7.2 0.8 fusion.176
  8.0 0.7 fusion.170
  8.7 0.7 convert_element_type.196
  9.4 1.6 fusion.39
  11.0 1.6 fusion.38
  12.6 2.3 fusion.41
  15.2 0.9 copy.26
  16.1 18.6 %all-gather.6.cloned.1.call-done = bf16[512,1024]{1,0:T(8,128)(2,1)} async-done(((bf16[512,256]{1,0:T(8,128)(2,1)}), bf16[512,1024]{1,0:T(8,128)(2,1)}) %all-gather.6.cloned.1.call-update) | async-done | bytes 1048592 | tf_op jit(solution)/shard_map/all_gather | solution.py:128
  34.6 1.5 convert_reduce_fusion
  36.2 1.6 fusion.24
  38.1 1.4 convolution_convert_fusion.2
  40.1 16.0 %all_gather.23 = bf16[2048,128]{0,1:T(8,128)(2,1)S(1)} all-gather(bf16[512,128]{0,1:T(8,128)(2,1)S(1)} %bitcast.157), channel_id=1, replica_groups=mesh['groups'=2,'seq'=4,'head'=2,'sub'=2] {'seq'}, dimensions={0}, use_global_device_ids=true | all-gather | bytes 655360 | tf_op jit(solution)/shard_map/all_gather | solution.py:151
  56.1 1.2 reshape_reshape.7
  57.3 1.9 copy.28
  59.2 2.1 multiply_reduce_fusion.5
  61.4 16.1 %all_gather.22 = bf16[2048,128]{1,0:T(8,128)(2,1)S(1)} all-gather(bf16[512,128]{1,0:T(8,128)(2,1)S(1)} %convolution_convert_fusion.2), channel_id=1, replica_groups=mesh['groups'=2,'seq'=4,'head'=2,'sub'=2] {'seq'}, dimensions={0}, use_global_device_ids=true | all-gather | bytes 655360 | tf_op jit(solution)/shard_map/all_gather | solution.py:152
  77.9 0.7 copy.27
  78.6 1.0 multiply_convert_fusion.5
  79.6 15.6 %while.15 = (s32[]{:T(128)}, f32[512,2,64]{0,2,1:T(8,128)S(1)}, f32[512,2]{0,1:T(2,128)S(1)}, bf16[4,512,2,64]{1,3,2,0:T(8,128)(2,1)S(1)}, s32[4]{0:T(128)S(1)},...) while((s32[]{:T(128)}, f32[512,2,64]{0,2,1:T(8,128)S(1)}, ...), condition=%wide.region_6.7_spmd.clone, body=%wide.region_4.6_spmd.clone.sunk | while | flops 136972288 | bytes 3032748 | solution.py:178
  79.6 0.6 dynamic_slice.49
  80.9 0.7 add_compare_fusion.2
  81.5 1.6 bitcast_reduce_fusion.2
  83.6 0.6 dynamic_slice.49
  84.8 0.7 add_compare_fusion.2
  85.5 1.6 bitcast_reduce_fusion.2
  87.5 0.6 dynamic_slice.49
  88.7 0.7 add_compare_fusion.2
  89.4 1.6 bitcast_reduce_fusion.2
  91.4 0.6 dynamic_slice.49
  92.6 0.7 add_compare_fusion.2
  93.3 1.6 bitcast_reduce_fusion.2
  95.3 2.4 convolution_convert_fusion.1
  97.9 36.0 %all-reduce.2.cloned.1.call-done = bf16[512,1024]{1,0:T(8,128)(2,1)} async-done(((bf16[512,1024]{1,0:T(8,128)(2,1)}), bf16[512,1024]{1,0:T(8,128)(2,1)}) %all-reduce.2.cloned.1.call-update) | async-done | bytes 1048592 | tf_op jit(solution)/shard_map/psum | solution.py:188
  133.9 1.7 fusion.26
  135.6 3.4 %collective-permute-start = (bf16[20,1024]{1,0:T(8,128)(2,1)S(1)}, bf16[20,1024]{1,0:T(8,128)(2,1)S(1)}, u32[]{:S(2)}, u32[]{:S(2)}) collective-permute-start(bf16[20,1024]{1,0:T(8,128)(2,1)S(1)} %get-tuple-element.190), channel_id=1, source_target_pairs={{0,4},{4,8},{8,12},{1,5},{5,9},{9,13},{2,6},{6,10},{10,14},{3,7},{... | collective-permute-start | bytes 122888 | tf_op jit(solution)/shard_map/ppermute | solution.py:17
  139.0 1.3 collective-permute-start.1
  140.8 4.3 %collective-permute-done.1 = bf16[20,1024]{1,0:T(8,128)(2,1)S(1)} collective-permute-done((bf16[20,1024]{1,0:T(8,128)(2,1)S(1)}, bf16[20,1024]{1,0:T(8,128)(2,1)S(1)}, u32[]{:S(2)}, u32[]{:S(2)}) %collective-permute-start.1) | collective-permute-done | bytes 40992 | tf_op jit(solution)/shard_map/ppermute | solution.py:18
  145.4 0.6 multiply_reduce_fusion
  146.1 0.7 fusion.34
  146.8 0.7 fusion.40
  147.6 2.3 multiply_convert_fusion.2
  149.9 1.5 convolution_convert_fusion
  151.5 0.5 all-gather.8.cloned.1.call-update
  152.1 0.5 all-gather.10.cloned.1.call-update
  152.7 0.5 all-gather.12.cloned.1.call-update
  155.0 15.1 %multiply_select_fusion = (f32[641,1280]{1,0:T(8,128)}, f32[641,1280]{1,0:T(8,128)}) fusion(f32[641]{0:T(1024)S(1)} %fusion.133, pred[641]{0:T(1024)(128)(4,1)S(1)} %fusion.132, f32[641]{0:T(1024)S(1)} %select_multiply_fusion), kind=kLoop, calls=%fused_computation.20 | loop fusion | flops 9845760 | bytes 6569609 | tf_op jit(solution)/shard_map/jit(_where)/select_n | solution.py:86
  170.1 1.8 fusion.166
  171.9 4.9 %reduce-scatter.2.cloned.1.call-done = bf16[1,138,1024]{2,1,0:T(8,128)(2,1)} async-done(((bf16[4,138,1024]{2,1,0:T(8,128)(2,1)}), bf16[1,138,1024]{2,1,0:T(8,128)(2,1)}) %reduce-scatter.2.cloned.1.call-update) | async-done | bytes 282640 | tf_op jit(solution)/shard_map/reduce_scatter | solution.py:210
  176.8 1.3 fusion.124
  178.1 1.4 multiply_reduce_fusion.1
  179.6 1.3 multiply_convert_fusion.1
  180.9 14.1 %all-gather.8.cloned.1.call-done = bf16[1024,512]{1,0:T(8,128)(2,1)} async-done(((bf16[256,512]{1,0:T(8,128)(2,1)}), bf16[1024,512]{1,0:T(8,128)(2,1)}) %all-gather.8.cloned.1.call-update) | async-done | bytes 1048592 | tf_op jit(solution)/shard_map/all_gather | solution.py:129
  194.9 1.7 fusion.177
  197.3 0.8 slice.454
  198.3 17.7 %all-gather.10.cloned.1.call-done = bf16[512,1536]{1,0:T(8,128)(2,1)} async-done(((bf16[128,1536]{1,0:T(8,128)(2,1)}), bf16[512,1536]{1,0:T(8,128)(2,1)}) %all-gather.10.cloned.1.call-update) | async-done | bytes 1572880 | tf_op jit(solution)/shard_map/all_gather | solution.py:130
  216.0 21.1 %all-gather.12.cloned.1.call-done = bf16[1536,512]{1,0:T(8,128)(2,1)} async-done(((bf16[384,512]{1,0:T(8,128)(2,1)}), bf16[1536,512]{1,0:T(8,128)(2,1)}) %all-gather.12.cloned.1.call-update) | async-done | bytes 1572880 | tf_op jit(solution)/shard_map/all_gather | solution.py:131
  237.1 4.3 %fusion.178 = (f32[132]{0:T(256)S(1)}, f32[132,512]{1,0:T(8,128)S(1)}) fusion(bf16[1536,512]{1,0:T(8,128)(2,1)} %all-gather.12.cloned.1.call-done, bf16[512,1536]{1,0:T(8,128)(2,1)} %all-gather.10.cloned.1.call-done, f32[132,512]{1,0:T(8,128)S(1)} %get-tuple-element.185, f32[132]{0:T(256)S(1)} %add_rsqrt_fusion.5, f32[132]{0:T(256)S(1)} %broadcast_multiply_fusion.4, ...), kind=kOutput, calls=%fused_computation.260 | convolution fusion | flops 428752768 | bytes 3958320 | tf_op jit(solution)/shard_map/dot_general | solution.py:229
  241.6 15.4 %all-gather.14.cloned.1.call-done = bf16[512,1282]{0,1:T(8,128)(2,1)} async-done(((bf16[128,1282]{0,1:T(8,128)(2,1)}), bf16[512,1282]{0,1:T(8,128)(2,1)}) %all-gather.14.cloned.1.call-update) | async-done | bytes 1312784 | tf_op jit(solution)/shard_map/all_gather | solution.py:132
  257.0 2.1 convolution_add_fusion
  259.2 1.9 cosine_multiply_fusion.1
  261.1 6.2 %fusion.19 = f32[132,1280]{1,0:T(8,128)S(1)} fusion(f32[641,1280]{1,0:T(8,128)S(1)} %copy-done.2, f32[641,1280]{1,0:T(8,128)} %get-tuple-element.254, f32[132,641]{1,0:T(8,128)S(1)} %get-tuple-element.199, f32[132,641]{1,0:T(8,128)S(1)} %get-tuple-element.198, f32[132]{0:T(256)S(1)} %and_convert_fusion, f32[1280]{0:T(1024)S(1)} %multiply_subtract_fusion), kind=kOutput, calls=%fused_computation.31 | convolution fusion | flops 2601428736 | bytes 7922224 | tf_op jit(solution)/shard_map/dot_general | solution.py:240
  267.3 0.6 reshape.181
  267.9 0.6 fusion.172
  268.6 0.8 div.84
  (83 shorter events, 6.3 us)
Async XLA Ops:
  7.2 142.8 %copy-start = (bf16[256,1024]{1,0:T(8,128)(2,1)S(1)}, bf16[256,1024]{1,0:T(8,128)(2,1)}, u32[]{:S(2)}) copy-start(bf16[256,1024]{1,0:T(8,128)(2,1)} %param.29) | copy-start | bytes 1572868
  7.2 27.5 %all-gather.6.cloned.1.call-start = ((), (), s32[]{:S(2)}) async-start(), calls=%async_computation.1 | async-start | bytes 1310720 | tf_op jit(solution)/shard_map/all_gather | solution.py:128
  11.0 4.1 %copy-start.3 = (bf16[3,1024,128]{2,1,0:T(8,128)(2,1)S(1)}, bf16[3,1024,128]{2,1,0:T(8,128)(2,1)}, u32[]{:S(2)}) copy-start(bf16[3,1024,128]{2,1,0:T(8,128)(2,1)} %param.24) | copy-start | bytes 2359300
  14.9 119.0 %all-reduce.2.cloned.1.call-start = ((), (), s32[]{:S(2)}) async-start(), calls=%async_computation.2 | async-start | bytes 2097152 | tf_op jit(solution)/shard_map/psum | solution.py:188
  34.6 3.2 %copy-start.1 = (bf16[512,1024]{1,0:T(8,128)(2,1)S(1)}, bf16[512,1024]{1,0:T(8,128)(2,1)}, u32[]{:S(2)}) copy-start(bf16[512,1024]{1,0:T(8,128)(2,1)} %all-gather.6.cloned.1.call-done) | copy-start | bytes 3145732
  61.4 18.3 %copy-start.8 = (f32[2]{0:T(128)S(1)}, f32[2]{0:T(128)}, u32[]{:S(2)}) copy-start(f32[2]{0:T(128)} %param.25) | copy-start | bytes 28
  95.3 2.6 copy-start.4
  97.8 79.0 %reduce-scatter.2.cloned.1.call-start = ((), (), s32[]{:S(2)}) async-start(), calls=%async_computation.3 | async-start | bytes 1474560 | tf_op jit(solution)/shard_map/reduce_scatter | solution.py:210
  133.9 12.1 %copy-start.7 = (bf16[2,1024,256]{2,1,0:T(8,128)(2,1)S(1)}, bf16[2,1024,256]{2,1,0:T(8,128)(2,1)}, u32[]{:S(2)}) copy-start(bf16[2,1024,256]{2,1,0:T(8,128)(2,1)} %param.27) | copy-start | bytes 3145732
  135.6 5.1 %collective-permute-start = (bf16[20,1024]{1,0:T(8,128)(2,1)S(1)}, bf16[20,1024]{1,0:T(8,128)(2,1)S(1)}, u32[]{:S(2)}, u32[]{:S(2)}) collective-permute-start(bf16[20,1024]{1,0:T(8,128)(2,1)S(1)} %get-tuple-element.190), channel_id=1, source_target_pairs={{0,4},{4,8},{8,12},{1,5},{5,9},{9,13},{2,6},{6,10},{10,14},{3,7},{... | collective-permute-start | bytes 122888 | tf_op jit(solution)/shard_map/ppermute | solution.py:17
  139.0 6.0 %collective-permute-start.1 = (bf16[20,1024]{1,0:T(8,128)(2,1)S(1)}, bf16[20,1024]{1,0:T(8,128)(2,1)S(1)}, u32[]{:S(2)}, u32[]{:S(2)}) collective-permute-start(bf16[20,1024]{1,0:T(8,128)(2,1)S(1)} %get-tuple-element.191), channel_id=1, source_target_pairs={{4,0},{8,4},{12,8},{5,1},{9,5},{13,9},{6,2},{10,6},{14,10},{7,3},{... | collective-permute-start | bytes 122888 | tf_op jit(solution)/shard_map/ppermute | solution.py:18
  149.9 4.8 %copy-start.5 = (f32[7,512]{1,0:T(8,128)S(1)}, f32[7,512]{1,0:T(8,128)}, u32[]{:S(2)}) copy-start(f32[7,512]{1,0:T(8,128)} %param.31) | copy-start | bytes 43012
  151.5 43.5 %all-gather.8.cloned.1.call-start = ((), (), s32[]{:S(2)}) async-start(), calls=%async_computation.4 | async-start | bytes 1310720 | tf_op jit(solution)/shard_map/all_gather | solution.py:129
  152.0 64.0 %all-gather.10.cloned.1.call-start = ((), (), s32[]{:S(2)}) async-start(), calls=%async_computation.5 | async-start | bytes 1966080 | tf_op jit(solution)/shard_map/all_gather | solution.py:130
  152.6 84.5 %all-gather.12.cloned.1.call-start = ((), (), s32[]{:S(2)}) async-start(), calls=%async_computation.6 | async-start | bytes 1966080 | tf_op jit(solution)/shard_map/all_gather | solution.py:131
  153.2 103.8 %all-gather.14.cloned.1.call-start = ((), (), s32[]{:S(2)}) async-start(), calls=%async_computation.7 | async-start | bytes 1648640 | tf_op jit(solution)/shard_map/all_gather | solution.py:132
  198.3 58.8 %copy-start.6 = (f32[1282]{0:T(1024)S(1)}, f32[1282]{0:T(1024)}, u32[]{:S(2)}) copy-start(f32[1282]{0:T(1024)} %param.35) | copy-start | bytes 15388
  257.0 4.0 %copy-start.2 = (f32[641,1280]{1,0:T(8,128)S(1)}, f32[641,1280]{1,0:T(8,128)}, u32[]{:S(2)}) copy-start(f32[641,1280]{1,0:T(8,128)} %get-tuple-element.253) | copy-start | bytes 9845764
Sparse Core Ops, SparseCore 0:
  15.1 19.5 all-gather.5
  97.9 35.9 all-reduce.1
  151.6 25.1 reduce-scatter.1
  178.2 16.6 all-gather.7
  196.3 19.6 all-gather.9
  217.4 19.6 all-gather.11
  238.6 18.3 all-gather.13
where the time goes:
time: 277 us; the launch traced here: 276 us
  waiting for transfers between devices  135 us (49%)
  other arithmetic  38 us (14%)
  matrix products  37 us (13%)
  blocking collectives  32.1 us (12%)
  between operations  15.2 us (5%)
  local copies, waits for them, and re-layouts  11.3 us (4%)
  starting transfers between devices  5.14 us (2%)
  loops' own time  2.77 us (1%)
    psum x1, waiting for transfers between devices, local(): lax.psum(head_part.astype(jnp.bfloat16), ('head', 'sub'))  36 us
    all_gather x1, waiting for transfers between devices, local(): lax.all_gather(voc_down, ('head', 'sub'), axis=0, tiled=True)  21.1 us
    all_gather x1, waiting for transfers between devices, local(): lax.all_gather(embedded, ('head', 'sub'), axis=1, tiled=True)  18.6 us
    all_gather x1, waiting for transfers between devices, local(): lax.all_gather(voc_up, ('head', 'sub'), axis=0, tiled=True)  17.7 us
    all_gather x1, blocking collectives, local(): value_piece = lax.all_gather(value_rows, 'seq', axis=0, tiled=True)  16.1 us
    all_gather x1, blocking collectives, local(): key_piece = lax.all_gather(key_unit, 'seq', axis=0, tiled=True)  16 us
    all_gather x1, waiting for transfers between devices, local(): lax.all_gather(voc_head, ('head', 'sub'), axis=0, tiled=True)  15.4 us
    select_n x1, other arithmetic, synthesis_tables(): sin_table = jnp.where(edge_bin, 0.0, -factor * jnp.sin(phase_angle))  15.1 us
  transfers between devices with their start and end apart: 9, of which 9 were waited for; matrix products, arithmetic and copies ran while one was open for 11% of the time, Pallas kernels for 0%

commit v1 on v0

--- a/solution.py
+++ b/solution.py
@@ -1,3 +1,4 @@
+import functools
 import math
 import jax
 import jax.numpy as jnp
@@ -5,6 +6,14 @@
 from jax.sharding import PartitionSpec as P
 
 HOP = 320
+
+
+def _attach_body(piece_in, mesh_name):
+    piece_now = jnp.sum(lax.all_gather(piece_in, mesh_name), axis=0)
+    return piece_now
+
+
+read_loads = functools.partial(_attach_body, mesh_name=("head", "sub"))
 
 
 def with_halo(x, sides, width):
@@ -185,9 +194,9 @@
     vocoder_rim = half_voc + intersection // 2
     conv_reach = conv_kernel.shape[0] // 2 + vocoder_rim
     window_rows = slab_rows + 2 * vocoder_rim
-    stream = inputs.astype(jnp.float32) + lax.psum(
-        head_part.astype(jnp.bfloat16), ("head", "sub")
-    ).astype(jnp.float32)
+    stream = inputs.astype(jnp.float32) + read_loads(head_part.astype(jnp.bfloat16)).astype(
+        jnp.float32
+    )
     stream_rims = with_halo(stream.astype(jnp.bfloat16), (("seq", 0),), conv_reach).astype(
         stream.dtype
     )

time: 277 us -> 279 us (level)
  other arithmetic: 38 us -> 42.4 us
  waiting for transfers between devices: 135 us -> 132 us
    psum x1 -> x0, waiting for transfers between devices: 36 us -> none  [local(): lax.psum(head_part.astype(jnp.bfloat16), ('head', 'sub'))]
    all_gather x0 -> x1, waiting for transfers between devices: none -> 34.2 us  [_attach_body(): piece_now = jnp.sum(lax.all_gather(piece_in, mesh_name), axis=0)]
    reduce_sum x0 -> x1, other arithmetic: none -> 4.39 us  [_attach_body(): piece_now = jnp.sum(lax.all_gather(piece_in, mesh_name), axis=0)]
where the time goes in v1:
time: 279 us; the launch traced here: 278 us
  waiting for transfers between devices  132 us (47%)
  other arithmetic  42.4 us (15%)
  matrix products  37 us (13%)
  blocking collectives  32.1 us (12%)
  between operations  15.2 us (5%)
  local copies, waits for them, and re-layouts  11.3 us (4%)
  starting transfers between devices  5.14 us (2%)
    all_gather x1, waiting for transfers between devices, _attach_body(): piece_now = jnp.sum(lax.all_gather(piece_in, mesh_name), axis=0)  34.2 us
    all_gather x1, waiting for transfers between devices, local(): lax.all_gather(voc_down, ('head', 'sub'), axis=0, tiled=True)  21.1 us
    all_gather x1, waiting for transfers between devices, local(): lax.all_gather(embedded, ('head', 'sub'), axis=1, tiled=True)  18.6 us
    all_gather x1, waiting for transfers between devices, local(): lax.all_gather(voc_up, ('head', 'sub'), axis=0, tiled=True)  17.7 us
    all_gather x1, blocking collectives, local(): value_piece = lax.all_gather(value_rows, 'seq', axis=0, tiled=True)  16.1 us
    all_gather x1, blocking collectives, local(): key_piece = lax.all_gather(key_unit, 'seq', axis=0, tiled=True)  16 us
    all_gather x1, waiting for transfers between devices, local(): lax.all_gather(voc_head, ('head', 'sub'), axis=0, tiled=True)  15.4 us
    select_n x1, other arithmetic, synthesis_tables(): sin_table = jnp.where(edge_bin, 0.0, -factor * jnp.sin(phase_angle))  15.1 us
  transfers between devices with their start and end apart: 9, of which 9 were waited for; matrix products, arithmetic and copies ran while one was open for 11% of the time, Pallas kernels for 0%

profile of v1, /device:TPU:0, one launch (start us, length us, event | category | flops | bytes accessed | tf_op | source)
XLA Modules:
  0.0 278.2 jit_solution(5725965116289755121)
XLA Ops:
  7.2 0.8 fusion.176
  8.0 0.7 fusion.170
  8.7 0.7 convert_element_type.198
  9.4 1.6 fusion.39
  11.0 1.6 fusion.38
  12.6 2.3 fusion.41
  15.2 0.9 copy.26
  16.1 18.6 %all-gather.8.cloned.1.call-done = bf16[512,1024]{1,0:T(8,128)(2,1)} async-done(((bf16[512,256]{1,0:T(8,128)(2,1)}), bf16[512,1024]{1,0:T(8,128)(2,1)}) %all-gather.8.cloned.1.call-update) | async-done | bytes 1048592 | tf_op jit(solution)/shard_map/all_gather | solution.py:137
  34.6 1.5 convert_reduce_fusion
  36.2 1.6 fusion.24
  38.1 1.4 convolution_convert_fusion.2
  40.1 16.0 %all_gather.29 = bf16[2048,128]{0,1:T(8,128)(2,1)S(1)} all-gather(bf16[512,128]{0,1:T(8,128)(2,1)S(1)} %bitcast.159), channel_id=1, replica_groups=mesh['groups'=2,'seq'=4,'head'=2,'sub'=2] {'seq'}, dimensions={0}, use_global_device_ids=true | all-gather | bytes 655360 | tf_op jit(solution)/shard_map/all_gather | solution.py:160
  56.1 1.2 reshape_reshape.7
  57.3 1.9 copy.28
  59.2 2.1 multiply_reduce_fusion.5
  61.4 16.1 %all_gather.28 = bf16[2048,128]{1,0:T(8,128)(2,1)S(1)} all-gather(bf16[512,128]{1,0:T(8,128)(2,1)S(1)} %convolution_convert_fusion.2), channel_id=1, replica_groups=mesh['groups'=2,'seq'=4,'head'=2,'sub'=2] {'seq'}, dimensions={0}, use_global_device_ids=true | all-gather | bytes 655360 | tf_op jit(solution)/shard_map/all_gather | solution.py:161
  77.9 0.7 copy.27
  78.6 1.0 multiply_convert_fusion.5
  79.6 15.6 %while.15 = (s32[]{:T(128)}, f32[512,2,64]{0,2,1:T(8,128)S(1)}, f32[512,2]{0,1:T(2,128)S(1)}, bf16[4,512,2,64]{1,3,2,0:T(8,128)(2,1)S(1)}, s32[4]{0:T(128)S(1)},...) while((s32[]{:T(128)}, f32[512,2,64]{0,2,1:T(8,128)S(1)}, ...), condition=%wide.region_6.7_spmd.clone, body=%wide.region_4.6_spmd.clone.sunk | while | flops 136972288 | bytes 3032748 | solution.py:187
  79.6 0.6 dynamic_slice.49
  80.9 0.7 add_compare_fusion.2
  81.5 1.6 bitcast_reduce_fusion.2
  83.6 0.6 dynamic_slice.49
  84.8 0.7 add_compare_fusion.2
  85.5 1.6 bitcast_reduce_fusion.2
  87.5 0.6 dynamic_slice.49
  88.7 0.7 add_compare_fusion.2
  89.4 1.6 bitcast_reduce_fusion.2
  91.4 0.6 dynamic_slice.49
  92.6 0.7 add_compare_fusion.2
  93.3 1.6 bitcast_reduce_fusion.2
  95.3 2.4 convolution_convert_fusion.1
  97.8 34.2 %all-gather.18.cloned.1.call-done = bf16[2048,1024]{1,0:T(8,128)(2,1)} async-done(((bf16[512,1024]{1,0:T(8,128)(2,1)}), bf16[2048,1024]{1,0:T(8,128)(2,1)}) %all-gather.18.cloned.1.call-update) | async-done | bytes 4194320 | tf_op jit(solution)/shard_map/all_gather | solution.py:12
  132.0 4.4 %reduce_sum.154 = bf16[512,1024]{1,0:T(8,128)(2,1)} reduce(bf16[4,512,1024]{2,1,0:T(8,128)(2,1)} %bitcast.156, bf16[]{:T(256)} %constant.72.clone.1), dimensions={0}, to_apply=%region_7.8 | reduce | flops 1572864 | bytes 5242882 | tf_op jit(solution)/shard_map/reduce_sum | solution.py:12
  136.4 1.7 fusion.26
  138.1 3.4 %collective-permute-start = (bf16[20,1024]{1,0:T(8,128)(2,1)S(1)}, bf16[20,1024]{1,0:T(8,128)(2,1)S(1)}, u32[]{:S(2)}, u32[]{:S(2)}) collective-permute-start(bf16[20,1024]{1,0:T(8,128)(2,1)S(1)} %get-tuple-element.190), channel_id=1, source_target_pairs={{0,4},{4,8},{8,12},{1,5},{5,9},{9,13},{2,6},{6,10},{10,14},{3,7},{... | collective-permute-start | bytes 122888 | tf_op jit(solution)/shard_map/ppermute | solution.py:26
  141.5 1.5 collective-permute-start.1
  143.3 4.3 %collective-permute-done.1 = bf16[20,1024]{1,0:T(8,128)(2,1)S(1)} collective-permute-done((bf16[20,1024]{1,0:T(8,128)(2,1)S(1)}, bf16[20,1024]{1,0:T(8,128)(2,1)S(1)}, u32[]{:S(2)}, u32[]{:S(2)}) %collective-permute-start.1) | collective-permute-done | bytes 40992 | tf_op jit(solution)/shard_map/ppermute | solution.py:27
  147.9 0.6 multiply_reduce_fusion
  148.5 0.7 fusion.34
  149.3 0.7 fusion.40
  150.1 2.3 multiply_convert_fusion.2
  152.4 1.5 convolution_convert_fusion
  154.6 0.5 all-gather.12.cloned.1.call-update
  155.8 0.7 all-gather.16.cloned.1.call-update
  157.5 15.1 %multiply_select_fusion = (f32[641,1280]{1,0:T(8,128)}, f32[641,1280]{1,0:T(8,128)}) fusion(f32[641]{0:T(1024)S(1)} %fusion.133, pred[641]{0:T(1024)(128)(4,1)S(1)} %fusion.132, f32[641]{0:T(1024)S(1)} %select_multiply_fusion), kind=kLoop, calls=%fused_computation.20 | loop fusion | flops 9845760 | bytes 6569609 | tf_op jit(solution)/shard_map/jit(_where)/select_n | solution.py:95
  172.6 1.8 fusion.166
  174.4 4.4 %reduce-scatter.2.cloned.1.call-done = bf16[1,138,1024]{2,1,0:T(8,128)(2,1)} async-done(((bf16[4,138,1024]{2,1,0:T(8,128)(2,1)}), bf16[1,138,1024]{2,1,0:T(8,128)(2,1)}) %reduce-scatter.2.cloned.1.call-update) | async-done | bytes 282640 | tf_op jit(solution)/shard_map/reduce_scatter | solution.py:219
  178.8 1.3 fusion.124
  180.2 1.4 multiply_reduce_fusion.1
  181.6 1.3 multiply_convert_fusion.1
  182.9 14.1 %all-gather.10.cloned.1.call-done = bf16[1024,512]{1,0:T(8,128)(2,1)} async-done(((bf16[256,512]{1,0:T(8,128)(2,1)}), bf16[1024,512]{1,0:T(8,128)(2,1)}) %all-gather.10.cloned.1.call-update) | async-done | bytes 1048592 | tf_op jit(solution)/shard_map/all_gather | solution.py:138
  197.0 1.7 fusion.177
  199.3 0.8 slice.454
  200.3 17.7 %all-gather.12.cloned.1.call-done = bf16[512,1536]{1,0:T(8,128)(2,1)} async-done(((bf16[128,1536]{1,0:T(8,128)(2,1)}), bf16[512,1536]{1,0:T(8,128)(2,1)}) %all-gather.12.cloned.1.call-update) | async-done | bytes 1572880 | tf_op jit(solution)/shard_map/all_gather | solution.py:139
  218.0 21.1 %all-gather.14.cloned.1.call-done = bf16[1536,512]{1,0:T(8,128)(2,1)} async-done(((bf16[384,512]{1,0:T(8,128)(2,1)}), bf16[1536,512]{1,0:T(8,128)(2,1)}) %all-gather.14.cloned.1.call-update) | async-done | bytes 1572880 | tf_op jit(solution)/shard_map/all_gather | solution.py:140
  239.1 4.3 %fusion.178 = (f32[132]{0:T(256)S(1)}, f32[132,512]{1,0:T(8,128)S(1)}) fusion(bf16[1536,512]{1,0:T(8,128)(2,1)} %all-gather.14.cloned.1.call-done, bf16[512,1536]{1,0:T(8,128)(2,1)} %all-gather.12.cloned.1.call-done, f32[132,512]{1,0:T(8,128)S(1)} %get-tuple-element.185, f32[132]{0:T(256)S(1)} %add_rsqrt_fusion.5, f32[132]{0:T(256)S(1)} %broadcast_multiply_fusion.4, ...), kind=kOutput, calls=%fused_computation.260 | convolution fusion | flops 428752768 | bytes 3958320 | tf_op jit(solution)/shard_map/dot_general | solution.py:238
  243.6 15.4 %all-gather.16.cloned.1.call-done = bf16[512,1282]{0,1:T(8,128)(2,1)} async-done(((bf16[128,1282]{0,1:T(8,128)(2,1)}), bf16[512,1282]{0,1:T(8,128)(2,1)}) %all-gather.16.cloned.1.call-update) | async-done | bytes 1312784 | tf_op jit(solution)/shard_map/all_gather | solution.py:141
  259.1 2.1 convolution_add_fusion
  261.2 1.9 cosine_multiply_fusion.1
  263.1 6.2 %fusion.19 = f32[132,1280]{1,0:T(8,128)S(1)} fusion(f32[641,1280]{1,0:T(8,128)S(1)} %copy-done.2, f32[641,1280]{1,0:T(8,128)} %get-tuple-element.254, f32[132,641]{1,0:T(8,128)S(1)} %get-tuple-element.199, f32[132,641]{1,0:T(8,128)S(1)} %get-tuple-element.198, f32[132]{0:T(256)S(1)} %and_convert_fusion, f32[1280]{0:T(1024)S(1)} %multiply_subtract_fusion), kind=kOutput, calls=%fused_computation.31 | convolution fusion | flops 2601428736 | bytes 7922224 | tf_op jit(solution)/shard_map/dot_general | solution.py:249
  269.3 0.6 reshape.181
  269.9 0.6 fusion.172
  270.6 0.8 div.84
  (84 shorter events, 6.4 us)
Async XLA Ops:
  7.2 145.3 %copy-start = (bf16[256,1024]{1,0:T(8,128)(2,1)S(1)}, bf16[256,1024]{1,0:T(8,128)(2,1)}, u32[]{:S(2)}) copy-start(bf16[256,1024]{1,0:T(8,128)(2,1)} %param.29) | copy-start | bytes 1572868
  7.2 27.5 %all-gather.8.cloned.1.call-start = ((), (), s32[]{:S(2)}) async-start(), calls=%async_computation.1 | async-start | bytes 1310720 | tf_op jit(solution)/shard_map/all_gather | solution.py:137
  11.0 4.1 %copy-start.3 = (bf16[3,1024,128]{2,1,0:T(8,128)(2,1)S(1)}, bf16[3,1024,128]{2,1,0:T(8,128)(2,1)}, u32[]{:S(2)}) copy-start(bf16[3,1024,128]{2,1,0:T(8,128)(2,1)} %param.24) | copy-start | bytes 2359300
  14.9 117.1 %all-gather.18.cloned.1.call-start = ((), (), s32[]{:S(2)}) async-start(), calls=%async_computation.7 | async-start | bytes 5242880 | tf_op jit(solution)/shard_map/all_gather | solution.py:12
  34.6 3.2 %copy-start.1 = (bf16[512,1024]{1,0:T(8,128)(2,1)S(1)}, bf16[512,1024]{1,0:T(8,128)(2,1)}, u32[]{:S(2)}) copy-start(bf16[512,1024]{1,0:T(8,128)(2,1)} %all-gather.8.cloned.1.call-done) | copy-start | bytes 3145732
  61.4 18.3 %copy-start.8 = (f32[2]{0:T(128)S(1)}, f32[2]{0:T(128)}, u32[]{:S(2)}) copy-start(f32[2]{0:T(128)} %param.25) | copy-start | bytes 28
  95.3 2.5 copy-start.4
  97.7 81.1 %reduce-scatter.2.cloned.1.call-start = ((), (), s32[]{:S(2)}) async-start(), calls=%async_computation.2 | async-start | bytes 1474560 | tf_op jit(solution)/shard_map/reduce_scatter | solution.py:219
  136.4 12.1 %copy-start.7 = (bf16[2,1024,256]{2,1,0:T(8,128)(2,1)S(1)}, bf16[2,1024,256]{2,1,0:T(8,128)(2,1)}, u32[]{:S(2)}) copy-start(bf16[2,1024,256]{2,1,0:T(8,128)(2,1)} %param.27) | copy-start | bytes 3145732
  138.1 5.1 %collective-permute-start = (bf16[20,1024]{1,0:T(8,128)(2,1)S(1)}, bf16[20,1024]{1,0:T(8,128)(2,1)S(1)}, u32[]{:S(2)}, u32[]{:S(2)}) collective-permute-start(bf16[20,1024]{1,0:T(8,128)(2,1)S(1)} %get-tuple-element.190), channel_id=1, source_target_pairs={{0,4},{4,8},{8,12},{1,5},{5,9},{9,13},{2,6},{6,10},{10,14},{3,7},{... | collective-permute-start | bytes 122888 | tf_op jit(solution)/shard_map/ppermute | solution.py:26
  141.5 6.0 %collective-permute-start.1 = (bf16[20,1024]{1,0:T(8,128)(2,1)S(1)}, bf16[20,1024]{1,0:T(8,128)(2,1)S(1)}, u32[]{:S(2)}, u32[]{:S(2)}) collective-permute-start(bf16[20,1024]{1,0:T(8,128)(2,1)S(1)} %get-tuple-element.191), channel_id=1, source_target_pairs={{4,0},{8,4},{12,8},{5,1},{9,5},{13,9},{6,2},{10,6},{14,10},{7,3},{... | collective-permute-start | bytes 122888 | tf_op jit(solution)/shard_map/ppermute | solution.py:27
  152.4 4.8 %copy-start.5 = (f32[7,512]{1,0:T(8,128)S(1)}, f32[7,512]{1,0:T(8,128)}, u32[]{:S(2)}) copy-start(f32[7,512]{1,0:T(8,128)} %param.31) | copy-start | bytes 43012
  154.0 43.0 %all-gather.10.cloned.1.call-start = ((), (), s32[]{:S(2)}) async-start(), calls=%async_computation.3 | async-start | bytes 1310720 | tf_op jit(solution)/shard_map/all_gather | solution.py:138
  154.5 63.5 %all-gather.12.cloned.1.call-start = ((), (), s32[]{:S(2)}) async-start(), calls=%async_computation.4 | async-start | bytes 1966080 | tf_op jit(solution)/shard_map/all_gather | solution.py:139
  155.1 84.0 %all-gather.14.cloned.1.call-start = ((), (), s32[]{:S(2)}) async-start(), calls=%async_computation.5 | async-start | bytes 1966080 | tf_op jit(solution)/shard_map/all_gather | solution.py:140
  155.7 103.3 %all-gather.16.cloned.1.call-start = ((), (), s32[]{:S(2)}) async-start(), calls=%async_computation.6 | async-start | bytes 1648640 | tf_op jit(solution)/shard_map/all_gather | solution.py:141
  200.3 58.8 %copy-start.6 = (f32[1282]{0:T(1024)S(1)}, f32[1282]{0:T(1024)}, u32[]{:S(2)}) copy-start(f32[1282]{0:T(1024)} %param.35) | copy-start | bytes 15388
  259.1 4.0 %copy-start.2 = (f32[641,1280]{1,0:T(8,128)S(1)}, f32[641,1280]{1,0:T(8,128)}, u32[]{:S(2)}) copy-start(f32[641,1280]{1,0:T(8,128)} %get-tuple-element.253) | copy-start | bytes 9845764
Sparse Core Ops, SparseCore 0:
  15.1 19.5 all-gather.7
  97.8 34.1 all-gather.17
  154.1 24.6 reduce-scatter.1
  180.2 16.6 all-gather.9
  198.4 19.6 all-gather.11
  219.4 19.6 all-gather.13
  240.7 18.3 all-gather.15
